TPU v7x, 32 devices: a whole 2x2x4 slice. The times are simulated.
32 devices in a mesh: view: 4 (over z), cell: 8 (over y, x, core).
Axes of the slice: x: 2, y: 2, z: 4, core: 2. Of those that a mesh axis runs over, the one named last changes fastest.
Arguments:
- params: float32 [59, 65536], P(None, 'cell'), may hold values from -6.22 to 3.2, as said below
- camera: float32 [4, 11], P('view'), may hold values from -0.3 to 1536, as said below
- targets: float32 [4, 256, 3, 256], P('view', 'cell'), may hold values from 0 to 1
- send_blocks: int32 [4, 8, 8, 16], P('view', 'cell'), may hold values from 0 to 255, as said below
- tile_blocks: int32 [4, 256, 16], P('view', 'cell'), may hold values from -1 to 127, as said below
- tile_order: int32 [4, 256, 512], P('view', 'cell'), may hold values from 0 to 511, as said below
Outputs:
- image: float32 [4, 256, 3, 256], P('view', 'cell')
- grads: float32 [59, 65536], P(None, 'cell')
Inputs may be any that keep to these rules, and one draw needn't show every extreme that they name: `params`: rows 0 to 2 lie in -3.2 to 3.2, rows 3 to 5 in log 0.002 to log 0.025, row 6 in 1 to 2, rows 7 to 9 in -1 to 1, row 10 in -3 to 2, rows 11 to 58 in -1.5 to 1.5. `camera`: quaternion first entry 1 to 2, its others -0.15 to 0.15, first two translation entries -0.3 to 0.3, third translation entry 4.5 to 6, focal lengths 2 to 3 times 16 max(32, 256 div 32), principal point within 20 of the image centre. `send_blocks`: the 16 numbers for one view, owner and receiving device are distinct. `tile_blocks`: A tile's live entries are distinct and come first, -1 fills the rest, and every tile has at least one live entry. `tile_order`: each tile's row is a permutation of 0 to 511.
All inputs are finite; a program needn't handle non-finite values.
Results may differ from a plain program's by a relative error of at most 0.0003.
Values sent between devices are 32-bit elements; how exact they have to be, the bound alone decides.
A program may use at most 128 MiB of HBM per device.

v0:
```python
import math
import jax
import jax.numpy as jnp
from jax import lax
from jax.sharding import PartitionSpec as P

BLOCK_GAUSSIANS = 32
TX = 32
HIGHEST_PRECISE = lax.Precision.HIGHEST
SH_ZERO = 0.28209479177387814
SH_ONE = 0.4886025119029199
SH_TWO = [
    1.0925484305920792,
    -1.0925484305920792,
    0.31539156525252005,
    -1.0925484305920792,
    0.5462742152960396,
]
SH_THREE = [
    -0.5900435899266435,
    2.890611442640554,
    -0.4570457994644658,
    0.3731763325901154,
    -0.4570457994644658,
    1.445305721320277,
    -0.5900435899266435,
]


def quat_matrix(qw, qx, qy, qz):
    return [
        [1.0 - 2.0 * (qy * qy + qz * qz), 2.0 * (qx * qy - qw * qz), 2.0 * (qx * qz + qw * qy)],
        [2.0 * (qx * qy + qw * qz), 1.0 - 2.0 * (qx * qx + qz * qz), 2.0 * (qy * qz - qw * qx)],
        [2.0 * (qx * qz - qw * qy), 2.0 * (qy * qz + qw * qx), 1.0 - 2.0 * (qx * qx + qy * qy)],
    ]


def sh_basis(dirx, diry, dirz):
    xx, yy, zz = (dirx * dirx, diry * diry, dirz * dirz)
    return [
        SH_ZERO + 0.0 * dirx,
        -SH_ONE * diry,
        SH_ONE * dirz,
        -SH_ONE * dirx,
        SH_TWO[0] * dirx * diry,
        SH_TWO[1] * diry * dirz,
        SH_TWO[2] * (2.0 * zz - xx - yy),
        SH_TWO[3] * dirx * dirz,
        SH_TWO[4] * (xx - yy),
        SH_THREE[0] * diry * (3.0 * xx - yy),
        SH_THREE[1] * dirx * diry * dirz,
        SH_THREE[2] * diry * (4.0 * zz - xx - yy),
        SH_THREE[3] * dirz * (2.0 * zz - 3.0 * xx - 3.0 * yy),
        SH_THREE[4] * dirx * (4.0 * zz - xx - yy),
        SH_THREE[5] * dirz * (xx - yy),
        SH_THREE[6] * dirx * (xx - 3.0 * yy),
    ]


def project(gauss, camera_row):
    cam_norm = jnp.sqrt(jnp.sum(camera_row[0:4] * camera_row[0:4]))
    cam_quat = camera_row[0:4] / cam_norm
    rotation = quat_matrix(cam_quat[0], cam_quat[1], cam_quat[2], cam_quat[3])
    focal_x, focal_y, centre_x, centre_y = (
        camera_row[7],
        camera_row[8],
        camera_row[9],
        camera_row[10],
    )
    cam_pos = [
        rotation[i][0] * gauss[0]
        + rotation[i][1] * gauss[1]
        + rotation[i][2] * gauss[2]
        + camera_row[4 + i]
        for i in range(3)
    ]
    inverse = 1.0 / cam_pos[2]
    screen_u = focal_x * cam_pos[0] * inverse + centre_x
    screen_w = focal_y * cam_pos[1] * inverse + centre_y
    gauss_norm = jnp.sqrt(
        gauss[6] * gauss[6] + gauss[7] * gauss[7] + gauss[8] * gauss[8] + gauss[9] * gauss[9]
    )
    grot = quat_matrix(
        gauss[6] / gauss_norm, gauss[7] / gauss_norm, gauss[8] / gauss_norm, gauss[9] / gauss_norm
    )
    scales = [jnp.exp(gauss[3 + k]) for k in range(3)]
    axes_cam = [
        [
            rotation[i][0] * grot[0][k] + rotation[i][1] * grot[1][k] + rotation[i][2] * grot[2][k]
            for k in range(3)
        ]
        for i in range(3)
    ]
    row_one = [
        (
            focal_x * inverse * axes_cam[0][k]
            - focal_x * cam_pos[0] * inverse * inverse * axes_cam[2][k]
        )
        * scales[k]
        for k in range(3)
    ]
    row_two = [
        (
            focal_y * inverse * axes_cam[1][k]
            - focal_y * cam_pos[1] * inverse * inverse * axes_cam[2][k]
        )
        * scales[k]
        for k in range(3)
    ]
    entry_a = row_one[0] * row_one[0] + row_one[1] * row_one[1] + row_one[2] * row_one[2] + 0.3
    entry_b = row_one[0] * row_two[0] + row_one[1] * row_two[1] + row_one[2] * row_two[2]
    entry_c = row_two[0] * row_two[0] + row_two[1] * row_two[1] + row_two[2] * row_two[2] + 0.3
    determinant = entry_a * entry_c - entry_b * entry_b
    opacity = jax.nn.sigmoid(gauss[10])
    distance = jnp.sqrt(cam_pos[0] * cam_pos[0] + cam_pos[1] * cam_pos[1] + cam_pos[2] * cam_pos[2])
    direction = [
        (rotation[0][j] * cam_pos[0] + rotation[1][j] * cam_pos[1] + rotation[2][j] * cam_pos[2])
        / distance
        for j in range(3)
    ]
    basis = sh_basis(direction[0], direction[1], direction[2])
    colors = []
    for channel in range(3):
        accum = 0.5 + basis[0] * gauss[11 + channel]
        for order in range(1, 16):
            accum = accum + basis[order] * gauss[11 + 3 * order + channel]
        colors.append(jnp.maximum(accum, 0.0))
    return jnp.stack(
        [
            screen_u,
            screen_w,
            entry_c / determinant,
            -entry_b / determinant,
            entry_a / determinant,
            opacity,
        ]
        + colors
    )


def expand(blocks, order):
    tiles_n, width = blocks.shape
    visible = blocks >= 0
    slots = jnp.maximum(blocks, 0)
    inner_product = jnp.arange(BLOCK_GAUSSIANS, dtype=jnp.int32)
    positions = (slots[:, :, None] * BLOCK_GAUSSIANS + inner_product).reshape(
        tiles_n, width * BLOCK_GAUSSIANS
    )
    visible = jnp.broadcast_to(visible[:, :, None], (tiles_n, width, BLOCK_GAUSSIANS)).reshape(
        tiles_n, width * BLOCK_GAUSSIANS
    )
    positions = jnp.take_along_axis(positions, order, axis=1)
    visible = jnp.take_along_axis(visible, order, axis=1)
    return (positions, visible)


def composite(fields, positions, visible, goal, first_tile):
    count, length = positions.shape
    pixels = goal.shape[-1]
    group = math.gcd(count, 4)
    steps_n = count // group
    pixel_ids = jnp.arange(pixels, dtype=jnp.int32)
    offset_x = (pixel_ids % 16).astype(jnp.float32) + 0.5
    offset_y = (pixel_ids // 16).astype(jnp.float32) + 0.5

    def step(carry, item):
        indices, alive, wanted, number = item
        tiles = first_tile + number * group + jnp.arange(group, dtype=jnp.int32)
        pix_x = (tiles % TX * 16).astype(jnp.float32)[:, None] + offset_x
        pix_y = (tiles // TX * 16).astype(jnp.float32)[:, None] + offset_y
        weights_mask = alive.astype(jnp.float32)

        def render(local_part):
            delta_x = pix_x[:, None, :] - local_part[0][:, :, None]
            delta_y = pix_y[:, None, :] - local_part[1][:, :, None]
            power = (
                -0.5
                * (
                    local_part[2][:, :, None] * delta_x * delta_x
                    + local_part[4][:, :, None] * delta_y * delta_y
                )
                - local_part[3][:, :, None] * delta_x * delta_y
            )
            alpha_value = (local_part[5] * weights_mask)[:, :, None] * jnp.exp(power)
            logs = jnp.log1p(-alpha_value)
            transmit_factor = jnp.exp(jnp.cumsum(logs, axis=1) - logs)
            return jnp.einsum(
                "dal,jda->djl",
                alpha_value * transmit_factor,
                local_part[6:9],
                precision=HIGHEST_PRECISE,
            )

        local_part = fields[:, indices]
        color, pullback = jax.vjp(render, local_part)
        local_grad = pullback((color - wanted) / pixels)[0]
        carry = carry.at[:, indices.reshape(-1)].add(local_grad.reshape(local_grad.shape[0], -1))
        return (carry, color)

    items = (
        positions.reshape(steps_n, group, length),
        visible.reshape(steps_n, group, length),
        goal.reshape(steps_n, group, 3, pixels),
        jnp.arange(steps_n, dtype=jnp.int32),
    )
    total, colors = lax.scan(step, jnp.zeros_like(fields), items)
    return (colors.reshape(count, 3, pixels), total)


def local(params, camera, targets, send_blocks, tile_blocks, tile_order):
    cells = lax.axis_size("cell")
    cell_index = lax.axis_index("cell")
    camera_row = camera[0]
    values_n = params.shape[0]
    owned_blocks = params.shape[1] // BLOCK_GAUSSIANS
    per_peer = send_blocks.shape[3]
    width = per_peer * BLOCK_GAUSSIANS
    picks = send_blocks[0, 0].reshape(-1)
    chosen = jnp.take(
        params.reshape(values_n, owned_blocks, BLOCK_GAUSSIANS), picks, axis=1
    ).reshape(values_n, cells * width)
    positions, visible = expand(tile_blocks[0], tile_order[0])
    first_tile = cell_index * tile_blocks.shape[1]
    received = lax.all_to_all(
        chosen.reshape(values_n, cells, width), "cell", split_axis=1, concat_axis=1, tiled=True
    ).reshape(values_n, cells * width)
    arrived, pullback = jax.vjp(lambda gathered: project(gathered, camera_row), received)
    picture, field_grad = composite(arrived, positions, visible, targets[0], first_tile)
    slot_grad = pullback(field_grad)[0]
    sent_grad = lax.all_to_all(
        slot_grad.reshape(values_n, cells, width), "cell", split_axis=1, concat_axis=1, tiled=True
    ).reshape(values_n, cells * width)
    per_block = jnp.transpose(
        sent_grad.reshape(values_n, cells * per_peer, BLOCK_GAUSSIANS), (1, 0, 2)
    )
    summed = jax.ops.segment_sum(per_block, picks, num_segments=owned_blocks)
    summed = jnp.transpose(summed, (1, 0, 2)).reshape(values_n, owned_blocks * BLOCK_GAUSSIANS)
    total = lax.psum(summed, "view")
    return (picture[None], total)


def solution(mesh):
    return jax.shard_map(
        local,
        mesh=mesh,
        in_specs=(
            P(None, "cell"),
            P("view", None),
            P("view", "cell", None, None),
            P("view", "cell", None, None),
            P("view", "cell", None),
            P("view", "cell", None),
        ),
        out_specs=(P("view", "cell", None, None), P(None, "cell")),
        check_vma=False,
    )
```

profile of v0, /device:TPU:0, one launch (start us, length us, event | category | flops | bytes accessed | tf_op | source)
XLA Modules:
  0.0 1059.9 jit_solution(7028042116414189610)
XLA Ops:
  8.6 3.9 copy.133
  12.7 2.9 gather_fusion.1
  17.3 3.2 copy.134
  20.5 5.2 all-to-all-start
  39.2 137.9 %gather_fusion.3 = pred[16384]{0:T(1024)(128)(4,1)S(1)} fusion(pred[32,512]{1,0:T(8,128)(4,1)S(1)} %reshape.6814, s32[16384]{0:T(1024)S(1)} %bitcast.267), kind=kCustom, calls=%fused_computation.3 | custom fusion | bytes 163840 | tf_op jit(solution)/shard_map/jit(take_along_axis)/gather | solution.py:153
  177.6 129.5 %gather_fusion.2 = s32[16384]{0:T(1024)S(1)} fusion(s32[32,512]{1,0:T(8,128)S(1)} %broadcast_add_fusion.4, s32[16384]{0:T(1024)S(1)} %bitcast.268), kind=kCustom, calls=%fused_computation.2 | custom fusion | bytes 262144 | tf_op jit(solution)/shard_map/jit(take_along_axis)/gather | solution.py:152
  313.6 2.7 fusion.154
  331.4 563.3 %while.15 = (s32[]{:T(128)}, f32[9,4096]{0,1:T(8,128)}, f32[8,4,3,256]{3,2,1,0:T(4,128)}, s32[8,4,512]{2,1,0:T(4,128)}, f32[9,4096]{0,1:T(8,128)}, /*index=5*/pr...) while((s32[]{:T(128)}, f32[9,4096]{0,1:T(8,128)}, ...), condition=%wide.region_13.14_spmd.clone, body=%wide.region_1.13_spmd.clone.sunk | while | flops 240312416 | bytes 65026284 | solution.py:206
  346.5 7.0 gather_fusion
  358.4 4.7 fusion.184
  371.0 6.0 fusion.186
  377.0 9.6 fusion.187
  391.6 7.6 fusion.188
  400.8 12.2 %scatter_fusion = f32[9,4096]{0,1:T(8,128)S(1)} fusion(f32[9,4096]{0,1:T(8,128)S(1)} %copy-done.2, s32[2048]{0:T(1024)S(1)} %bitcast.313, f32[2048,9]{1,0:T(8,128)S(1)} %copy.228), kind=kCustom, calls=%fused_computation.4.clone.clone.1 | custom fusion | flops 18432 | bytes 229376 | tf_op jit(solution)/shard_map/while/body/eval_jaxpr/scatter-add | solution.py:197
  415.1 7.0 gather_fusion
  427.0 4.7 fusion.184
  439.6 6.0 fusion.186
  445.6 9.6 fusion.187
  460.2 7.6 fusion.188
  469.4 12.2 %scatter_fusion = f32[9,4096]{0,1:T(8,128)S(1)} fusion(f32[9,4096]{0,1:T(8,128)S(1)} %copy-done.2, s32[2048]{0:T(1024)S(1)} %bitcast.313, f32[2048,9]{1,0:T(8,128)S(1)} %copy.228), kind=kCustom, calls=%fused_computation.4.clone.clone.1 | custom fusion | flops 18432 | bytes 229376 | tf_op jit(solution)/shard_map/while/body/eval_jaxpr/scatter-add | solution.py:197
  483.7 7.0 gather_fusion
  495.6 4.7 fusion.184
  508.2 6.0 fusion.186
  514.3 9.6 fusion.187
  528.9 7.6 fusion.188
  538.0 12.2 %scatter_fusion = f32[9,4096]{0,1:T(8,128)S(1)} fusion(f32[9,4096]{0,1:T(8,128)S(1)} %copy-done.2, s32[2048]{0:T(1024)S(1)} %bitcast.313, f32[2048,9]{1,0:T(8,128)S(1)} %copy.228), kind=kCustom, calls=%fused_computation.4.clone.clone.1 | custom fusion | flops 18432 | bytes 229376 | tf_op jit(solution)/shard_map/while/body/eval_jaxpr/scatter-add | solution.py:197
  552.3 7.0 gather_fusion
  564.2 4.7 fusion.184
  576.8 6.0 fusion.186
  582.8 9.6 fusion.187
  597.4 7.6 fusion.188
  606.6 12.2 %scatter_fusion = f32[9,4096]{0,1:T(8,128)S(1)} fusion(f32[9,4096]{0,1:T(8,128)S(1)} %copy-done.2, s32[2048]{0:T(1024)S(1)} %bitcast.313, f32[2048,9]{1,0:T(8,128)S(1)} %copy.228), kind=kCustom, calls=%fused_computation.4.clone.clone.1 | custom fusion | flops 18432 | bytes 229376 | tf_op jit(solution)/shard_map/while/body/eval_jaxpr/scatter-add | solution.py:197
  620.9 7.0 gather_fusion
  632.8 4.7 fusion.184
  645.4 6.0 fusion.186
  651.4 9.6 fusion.187
  666.0 7.6 fusion.188
  675.2 12.2 %scatter_fusion = f32[9,4096]{0,1:T(8,128)S(1)} fusion(f32[9,4096]{0,1:T(8,128)S(1)} %copy-done.2, s32[2048]{0:T(1024)S(1)} %bitcast.313, f32[2048,9]{1,0:T(8,128)S(1)} %copy.228), kind=kCustom, calls=%fused_computation.4.clone.clone.1 | custom fusion | flops 18432 | bytes 229376 | tf_op jit(solution)/shard_map/while/body/eval_jaxpr/scatter-add | solution.py:197
  689.5 7.0 gather_fusion
  701.4 4.7 fusion.184
  714.1 6.0 fusion.186
  720.1 9.6 fusion.187
  734.7 7.6 fusion.188
  743.9 12.2 %scatter_fusion = f32[9,4096]{0,1:T(8,128)S(1)} fusion(f32[9,4096]{0,1:T(8,128)S(1)} %copy-done.2, s32[2048]{0:T(1024)S(1)} %bitcast.313, f32[2048,9]{1,0:T(8,128)S(1)} %copy.228), kind=kCustom, calls=%fused_computation.4.clone.clone.1 | custom fusion | flops 18432 | bytes 229376 | tf_op jit(solution)/shard_map/while/body/eval_jaxpr/scatter-add | solution.py:197
  758.1 7.0 gather_fusion
  770.0 4.7 fusion.184
  782.7 6.0 fusion.186
  788.7 9.6 fusion.187
  803.3 7.6 fusion.188
  812.5 12.2 %scatter_fusion = f32[9,4096]{0,1:T(8,128)S(1)} fusion(f32[9,4096]{0,1:T(8,128)S(1)} %copy-done.2, s32[2048]{0:T(1024)S(1)} %bitcast.313, f32[2048,9]{1,0:T(8,128)S(1)} %copy.228), kind=kCustom, calls=%fused_computation.4.clone.clone.1 | custom fusion | flops 18432 | bytes 229376 | tf_op jit(solution)/shard_map/while/body/eval_jaxpr/scatter-add | solution.py:197
  826.7 7.0 gather_fusion
  838.7 4.7 fusion.184
  851.3 6.0 fusion.186
  857.3 9.6 fusion.187
  871.9 7.6 fusion.188
  881.1 12.2 %scatter_fusion = f32[9,4096]{0,1:T(8,128)S(1)} fusion(f32[9,4096]{0,1:T(8,128)S(1)} %copy-done.2, s32[2048]{0:T(1024)S(1)} %bitcast.313, f32[2048,9]{1,0:T(8,128)S(1)} %copy.228), kind=kCustom, calls=%fused_computation.4.clone.clone.1 | custom fusion | flops 18432 | bytes 229376 | tf_op jit(solution)/shard_map/while/body/eval_jaxpr/scatter-add | solution.py:197
  910.2 3.9 broadcast_multiply_fusion.10
  916.1 3.4 fusion.80
  921.7 4.2 all-to-all-start.1
  926.1 15.2 %all-to-all-done.1 = f32[59,8,512]{2,0,1:T(8,128)S(1)} async-done(((f32[59,8,512]{2,0,1:T(8,128)}), f32[59,8,512]{2,0,1:T(8,128)S(1)}, u32[]{:S(2)}, u32[]{:S(2)}) %all-to-all-start.1) | async-done | bytes 966688 | tf_op jit(solution)/shard_map/all_to_all | solution.py:230
  944.5 15.5 %scatter_fusion.1 = f32[256,59,32]{1,2,0:T(8,128)} fusion(f32[256,59,32]{1,2,0:T(8,128)} %broadcast_in_dim.76, s32[128]{0:T(128)S(1)} %reshape.6864, f32[128,59,32]{1,2,0:T(8,128)S(1)} %bitcast.272), kind=kCustom, calls=%fused_computation.5 | custom fusion | flops 241664 | bytes 2900480 | tf_op jit(solution)/shard_map/scatter-add | solution.py:236
  960.0 3.8 copy.152
  965.4 84.2 %all-reduce.78.cloned.1.call-done = f32[59,8192]{1,0:T(8,128)} async-done(((f32[59,8192]{1,0:T(8,128)}), f32[59,8192]{1,0:T(8,128)}) %all-reduce.78.cloned.1.call-update) | async-done | bytes 1933328 | tf_op jit(solution)/shard_map/psum | solution.py:238
  1049.6 3.1 copy.244
  (961 shorter events, 213.1 us)
Async XLA Ops:
  17.3 8.4 copy-start.119
  17.3 8.5 copy-start.120
  17.3 9.8 copy-start.52
  20.5 289.3 %all-to-all-start = ((f32[59,8,512]{2,0,1:T(8,128)}), f32[59,8,512]{2,0,1:T(8,128)S(1)}, u32[]{:S(2)}, u32[]{:S(2)}) async-start(f32[59,8,512]{2,0,1:T(8,128)} %copy.134), calls=%async_computation | async-start | bytes 2097152 | tf_op jit(solution)/shard_map/all_to_all | solution.py:224
  177.6 129.5 %copy-start.117 = (f32[1,32,3,256]{3,1,2,0:T(8,128)S(1)}, f32[1,32,3,256]{3,1,2,0:T(8,128)}, u32[]{:S(2)}) copy-start(f32[1,32,3,256]{3,1,2,0:T(8,128)} %param.10) | copy-start | bytes 294916
  310.7 9.8 copy-start.53
  310.7 9.8 copy-start.55
  310.7 9.8 copy-start.57
  310.7 9.8 copy-start.59
  310.7 15.4 %copy-start.28 = (f32[1,8,512]{2,0,1:T(1,128)}, f32[1,8,512]{2,0,1:T(1,128)S(1)}, u32[]{:S(2)}) copy-start(f32[1,8,512]{2,0,1:T(1,128)S(1)} %get-tuple-element.415) | copy-start | bytes 49156
  312.3 10.5 copy-start.14
  313.6 9.1 copy-start.12
  313.6 12.6 %copy-start.50 = (f32[1,8,512]{2,0,1:T(1,128)}, f32[1,8,512]{2,0,1:T(1,128)S(1)}, u32[]{:S(2)}) copy-start(f32[1,8,512]{2,0,1:T(1,128)S(1)} %get-tuple-element.416) | copy-start | bytes 49156
  320.4 5.9 copy-start.77
  320.4 5.9 copy-start.79
  320.4 5.9 copy-start.81
  320.4 5.9 copy-start.83
  320.4 5.9 copy-start.85
  320.4 5.9 copy-start.87
  320.4 5.9 copy-start.89
  320.4 5.9 copy-start.91
  320.4 5.9 copy-start.93
  391.6 7.7 copy-start.31
  460.2 7.7 copy-start.31
  528.9 7.7 copy-start.31
  597.4 7.7 copy-start.31
  666.0 7.7 copy-start.31
  734.7 7.7 copy-start.31
  803.3 7.7 copy-start.31
  871.9 7.7 copy-start.31
  894.8 12.6 %copy-start.40 = (f32[1,4096]{1,0:T(1,128)S(1)}, f32[1,4096]{1,0:T(1,128)}, u32[]{:S(2)}) copy-start(f32[1,4096]{1,0:T(1,128)} %get-tuple-element.302) | copy-start | bytes 49156
  894.8 13.4 %copy-start.33 = (f32[1,4096]{1,0:T(1,128)S(1)}, f32[1,4096]{1,0:T(1,128)}, u32[]{:S(2)}) copy-start(f32[1,4096]{1,0:T(1,128)} %copy-done.32) | copy-start | bytes 49156
  894.8 13.4 %copy-start.35 = (f32[1,4096]{1,0:T(1,128)S(1)}, f32[1,4096]{1,0:T(1,128)}, u32[]{:S(2)}) copy-start(f32[1,4096]{1,0:T(1,128)} %copy-done.34) | copy-start | bytes 49156
  894.8 13.4 %copy-start.37 = (f32[1,4096]{1,0:T(1,128)S(1)}, f32[1,4096]{1,0:T(1,128)}, u32[]{:S(2)}) copy-start(f32[1,4096]{1,0:T(1,128)} %copy-done.36) | copy-start | bytes 49156
  894.8 13.4 %copy-start.39 = (f32[1,4096]{1,0:T(1,128)S(1)}, f32[1,4096]{1,0:T(1,128)}, u32[]{:S(2)}) copy-start(f32[1,4096]{1,0:T(1,128)} %copy-done.38) | copy-start | bytes 49156
  894.8 13.4 %copy-start.45 = (f32[1,4096]{1,0:T(1,128)S(1)}, f32[1,4096]{1,0:T(1,128)}, u32[]{:S(2)}) copy-start(f32[1,4096]{1,0:T(1,128)} %copy-done.44) | copy-start | bytes 49156
  894.8 13.4 %copy-start.47 = (f32[1,4096]{1,0:T(1,128)S(1)}, f32[1,4096]{1,0:T(1,128)}, u32[]{:S(2)}) copy-start(f32[1,4096]{1,0:T(1,128)} %copy-done.46) | copy-start | bytes 49156
  894.9 13.4 %copy-start.49 = (f32[1,4096]{1,0:T(1,128)S(1)}, f32[1,4096]{1,0:T(1,128)}, u32[]{:S(2)}) copy-start(f32[1,4096]{1,0:T(1,128)} %copy-done.48) | copy-start | bytes 49156
  897.1 12.8 %copy-start.41 = (f32[1,4096]{1,0:T(1,128)S(1)}, f32[1,4096]{1,0:T(1,128)}, u32[]{:S(2)}) copy-start(f32[1,4096]{1,0:T(1,128)} %get-tuple-element.321) | copy-start | bytes 49156
  897.1 12.8 %copy-start.42 = (f32[1,4096]{1,0:T(1,128)S(1)}, f32[1,4096]{1,0:T(1,128)}, u32[]{:S(2)}) copy-start(f32[1,4096]{1,0:T(1,128)} %get-tuple-element.327) | copy-start | bytes 49156
  897.1 12.8 %copy-start.43 = (f32[1,4096]{1,0:T(1,128)S(1)}, f32[1,4096]{1,0:T(1,128)}, u32[]{:S(2)}) copy-start(f32[1,4096]{1,0:T(1,128)} %get-tuple-element.333) | copy-start | bytes 49156
  897.2 12.8 %copy-start.51 = (f32[1,8,512]{2,0,1:T(1,128)S(1)}, f32[1,8,512]{2,0,1:T(1,128)}, u32[]{:S(2)}) copy-start(f32[1,8,512]{2,0,1:T(1,128)} %copy-done.50) | copy-start | bytes 49156
  897.2 12.8 %copy-start.70 = (f32[1,8,512]{2,0,1:T(1,128)S(1)}, f32[1,8,512]{2,0,1:T(1,128)}, u32[]{:S(2)}) copy-start(f32[1,8,512]{2,0,1:T(1,128)} %copy-done.69) | copy-start | bytes 49156
  897.2 12.8 %copy-start.72 = (f32[1,8,512]{2,0,1:T(1,128)S(1)}, f32[1,8,512]{2,0,1:T(1,128)}, u32[]{:S(2)}) copy-start(f32[1,8,512]{2,0,1:T(1,128)} %copy-done.71) | copy-start | bytes 49156
  897.2 12.8 %copy-start.74 = (f32[1,8,512]{2,0,1:T(1,128)S(1)}, f32[1,8,512]{2,0,1:T(1,128)}, u32[]{:S(2)}) copy-start(f32[1,8,512]{2,0,1:T(1,128)} %copy-done.73) | copy-start | bytes 49156
  897.2 12.8 %copy-start.76 = (f32[1,8,512]{2,0,1:T(1,128)S(1)}, f32[1,8,512]{2,0,1:T(1,128)}, u32[]{:S(2)}) copy-start(f32[1,8,512]{2,0,1:T(1,128)} %copy-done.75) | copy-start | bytes 49156
  897.2 12.8 %copy-start.78 = (f32[1,8,512]{2,0,1:T(1,128)S(1)}, f32[1,8,512]{2,0,1:T(1,128)}, u32[]{:S(2)}) copy-start(f32[1,8,512]{2,0,1:T(1,128)} %copy-done.77) | copy-start | bytes 49156
  897.2 12.8 %copy-start.80 = (f32[1,8,512]{2,0,1:T(1,128)S(1)}, f32[1,8,512]{2,0,1:T(1,128)}, u32[]{:S(2)}) copy-start(f32[1,8,512]{2,0,1:T(1,128)} %copy-done.79) | copy-start | bytes 49156
  897.2 12.8 %copy-start.82 = (f32[1,8,512]{2,0,1:T(1,128)S(1)}, f32[1,8,512]{2,0,1:T(1,128)}, u32[]{:S(2)}) copy-start(f32[1,8,512]{2,0,1:T(1,128)} %copy-done.81) | copy-start | bytes 49156
  897.2 12.8 %copy-start.84 = (f32[1,8,512]{2,0,1:T(1,128)S(1)}, f32[1,8,512]{2,0,1:T(1,128)}, u32[]{:S(2)}) copy-start(f32[1,8,512]{2,0,1:T(1,128)} %copy-done.83) | copy-start | bytes 49156
  897.2 12.8 %copy-start.86 = (f32[1,8,512]{2,0,1:T(1,128)S(1)}, f32[1,8,512]{2,0,1:T(1,128)}, u32[]{:S(2)}) copy-start(f32[1,8,512]{2,0,1:T(1,128)} %copy-done.85) | copy-start | bytes 49156
  897.3 12.8 %copy-start.88 = (f32[1,8,512]{2,0,1:T(1,128)S(1)}, f32[1,8,512]{2,0,1:T(1,128)}, u32[]{:S(2)}) copy-start(f32[1,8,512]{2,0,1:T(1,128)} %copy-done.87) | copy-start | bytes 49156
  897.3 12.8 %copy-start.90 = (f32[1,8,512]{2,0,1:T(1,128)S(1)}, f32[1,8,512]{2,0,1:T(1,128)}, u32[]{:S(2)}) copy-start(f32[1,8,512]{2,0,1:T(1,128)} %copy-done.89) | copy-start | bytes 49156
  897.3 12.8 %copy-start.92 = (f32[1,8,512]{2,0,1:T(1,128)S(1)}, f32[1,8,512]{2,0,1:T(1,128)}, u32[]{:S(2)}) copy-start(f32[1,8,512]{2,0,1:T(1,128)} %copy-done.91) | copy-start | bytes 49156
  897.3 12.8 %copy-start.94 = (f32[1,8,512]{2,0,1:T(1,128)S(1)}, f32[1,8,512]{2,0,1:T(1,128)}, u32[]{:S(2)}) copy-start(f32[1,8,512]{2,0,1:T(1,128)} %copy-done.93) | copy-start | bytes 49156
  898.4 9.9 copy-start.100
  898.4 11.7 %copy-start.96 = (f32[1,8,512]{2,0,1:T(1,128)S(1)}, f32[1,8,512]{2,0,1:T(1,128)}, u32[]{:S(2)}) copy-start(f32[1,8,512]{2,0,1:T(1,128)} %copy-done.95) | copy-start | bytes 49156
  898.4 11.7 %copy-start.98 = (f32[1,8,512]{2,0,1:T(1,128)S(1)}, f32[1,8,512]{2,0,1:T(1,128)}, u32[]{:S(2)}) copy-start(f32[1,8,512]{2,0,1:T(1,128)} %copy-done.97) | copy-start | bytes 49156
  898.4 11.7 %copy-start.101 = (f32[1,4096]{1,0:T(1,128)S(1)}, f32[1,4096]{1,0:T(1,128)}, u32[]{:S(2)}) copy-start(f32[1,4096]{1,0:T(1,128)} %get-tuple-element.297) | copy-start | bytes 49156
  899.4 10.8 %copy-start.102 = (f32[1,4096]{1,0:T(1,128)S(1)}, f32[1,4096]{1,0:T(1,128)}, u32[]{:S(2)}) copy-start(f32[1,4096]{1,0:T(1,128)} %get-tuple-element.300) | copy-start | bytes 49156
  900.4 9.8 copy-start.103
  900.4 9.8 copy-start.105
  921.7 19.6 %all-to-all-start.1 = ((f32[59,8,512]{2,0,1:T(8,128)}), f32[59,8,512]{2,0,1:T(8,128)S(1)}, u32[]{:S(2)}, u32[]{:S(2)}) async-start(f32[59,8,512]{2,0,1:T(8,128)} %copy.150), calls=%async_computation.1 | async-start | bytes 2097152 | tf_op jit(solution)/shard_map/all_to_all | solution.py:230
  925.9 123.6 %all-reduce.78.cloned.1.call-start = ((), (), s32[]{:S(2)}) async-start(), calls=%async_computation.2 | async-start | bytes 4194304 | tf_op jit(solution)/shard_map/psum | solution.py:238
  (186 other events, 448.9 us)
Sparse Core Ops, SparseCore 0:
  964.0 85.5 all-reduce.77
where the time goes:
time: 1070 us; the launch traced here: 1060 us
  local copies, waits for them, and re-layouts  444 us (41%)
  other arithmetic  374 us (35%)
  waiting for transfers between devices  99.4 us (9%)
  matrix products  82.1 us (8%)
  between operations  27.9 us (3%)
  loops' own time  23 us (2%)
    gather x2, local copies, waits for them, and re-layouts, expand(): visible = jnp.take_along_axis(visible, order, axis=1)  138 us
    another operation x48, other arithmetic  134 us
    gather x2, local copies, waits for them, and re-layouts, expand(): positions = jnp.take_along_axis(positions, order, axis=1)  129 us
    scatter-add x8, other arithmetic, step(): carry.at[:, indices.reshape(-1)]  97.8 us
    psum x1, waiting for transfers between devices, local(): total = lax.psum(summed, 'view')  84.2 us
    dot_general x24, matrix products, render(): jnp.einsum('dal,jda->djl', alpha_value * transmit_factor, local_part[6:9]...  82.1 us
    reduce_sum x8, other arithmetic, render(): local_part[3][:, :, None] * delta_x * delta_y  60.7 us
    gather x16, local copies, waits for them, and re-layouts, step(): local_part = fields[:, indices]  59 us
  transfers between devices with their start and end apart: 3, of which 2 were waited for; matrix products, arithmetic and copies ran while one was open for 26% of the time, Pallas kernels for 0%

commit v1 on v0

--- a/solution.py
+++ b/solution.py
@@ -235,7 +235,7 @@
     )
     summed = jax.ops.segment_sum(per_block, picks, num_segments=owned_blocks)
     summed = jnp.transpose(summed, (1, 0, 2)).reshape(values_n, owned_blocks * BLOCK_GAUSSIANS)
-    total = lax.psum(summed, "view")
+    total = jnp.sum(lax.all_gather(summed, "view"), axis=0)
     return (picture[None], total)
 
 

time: 1070 us -> 1140 us (1.065)
  waiting for transfers between devices: 99.4 us -> 163 us
    all_gather x0 -> x1, waiting for transfers between devices: none -> 148 us  [local(): total = jnp.sum(lax.all_gather(summed, 'view'), axis=0)]
    psum x1 -> x0, waiting for transfers between devices: 84.2 us -> none  [local(): total = lax.psum(summed, 'view')]
  transfers between devices with their start and end apart: 3 -> 3, of which waited for: 2 -> 2; matrix products, arithmetic and copies ran while one was open for 26% -> 24% of each run, Pallas kernels for 0% -> 0%
where the time goes in v1:
time: 1140 us; the launch traced here: 1130 us
  local copies, waits for them, and re-layouts  442 us (39%)
  other arithmetic  378 us (33%)
  waiting for transfers between devices  163 us (14%)
  matrix products  82.1 us (7%)
  between operations  28.2 us (2%)
  loops' own time  23.4 us (2%)
    all_gather x1, waiting for transfers between devices, local(): total = jnp.sum(lax.all_gather(summed, 'view'), axis=0)  148 us
    gather x2, local copies, waits for them, and re-layouts, expand(): visible = jnp.take_along_axis(visible, order, axis=1)  138 us
    another operation x48, other arithmetic  134 us
    gather x2, local copies, waits for them, and re-layouts, expand(): positions = jnp.take_along_axis(positions, order, axis=1)  129 us
    scatter-add x8, other arithmetic, step(): carry.at[:, indices.reshape(-1)]  97.8 us
    dot_general x24, matrix products, render(): jnp.einsum('dal,jda->djl', alpha_value * transmit_factor, local_part[6:9]...  82.1 us
    reduce_sum x8, other arithmetic, render(): local_part[3][:, :, None] * delta_x * delta_y  60.7 us
    gather x16, local copies, waits for them, and re-layouts, step(): local_part = fields[:, indices]  59 us
  transfers between devices with their start and end apart: 3, of which 2 were waited for; matrix products, arithmetic and copies ran while one was open for 24% of the time, Pallas kernels for 0%

profile of v1, /device:TPU:0, one launch (start us, length us, event | category | flops | bytes accessed | tf_op | source)
XLA Modules:
  0.0 1126.7 jit_solution(16010438619425450748)
XLA Ops:
  8.6 3.9 copy.135
  12.7 2.9 gather_fusion.1
  17.3 3.2 copy.136
  20.5 5.2 all-to-all-start
  39.5 137.9 %gather_fusion.3 = pred[16384]{0:T(1024)(128)(4,1)S(1)} fusion(pred[32,512]{1,0:T(8,128)(4,1)S(1)} %reshape.6811, s32[16384]{0:T(1024)S(1)} %bitcast.267), kind=kCustom, calls=%fused_computation.3 | custom fusion | bytes 163840 | tf_op jit(solution)/shard_map/jit(take_along_axis)/gather | solution.py:153
  177.9 129.5 %gather_fusion.2 = s32[16384]{0:T(1024)S(1)} fusion(s32[32,512]{1,0:T(8,128)S(1)} %broadcast_add_fusion.4, s32[16384]{0:T(1024)S(1)} %bitcast.268), kind=kCustom, calls=%fused_computation.2 | custom fusion | bytes 262144 | tf_op jit(solution)/shard_map/jit(take_along_axis)/gather | solution.py:152
  313.8 2.6 fusion.154
  331.5 564.7 %while.15 = (s32[]{:T(128)}, f32[9,4096]{0,1:T(8,128)}, f32[8,4,3,256]{3,2,1,0:T(4,128)}, s32[8,4,512]{2,1,0:T(4,128)}, f32[9,4096]{0,1:T(8,128)}, /*index=5*/pr...) while((s32[]{:T(128)}, f32[9,4096]{0,1:T(8,128)}, ...), condition=%wide.region_13.14_spmd.clone, body=%wide.region_1.13_spmd.clone.sunk | while | flops 240312416 | bytes 65026284 | solution.py:206
  346.5 7.0 gather_fusion
  358.6 4.7 fusion.184
  371.3 6.0 fusion.186
  377.3 9.6 fusion.187
  391.9 7.6 fusion.188
  401.1 12.2 %scatter_fusion = f32[9,4096]{0,1:T(8,128)S(1)} fusion(f32[9,4096]{0,1:T(8,128)S(1)} %copy-done.2, s32[2048]{0:T(1024)S(1)} %bitcast.313, f32[2048,9]{1,0:T(8,128)S(1)} %copy.233), kind=kCustom, calls=%fused_computation.4.clone.clone.1 | custom fusion | flops 18432 | bytes 229376 | tf_op jit(solution)/shard_map/while/body/eval_jaxpr/scatter-add | solution.py:197
  415.3 7.0 gather_fusion
  427.4 4.7 fusion.184
  440.0 6.0 fusion.186
  446.0 9.6 fusion.187
  460.7 7.6 fusion.188
  469.9 12.2 %scatter_fusion = f32[9,4096]{0,1:T(8,128)S(1)} fusion(f32[9,4096]{0,1:T(8,128)S(1)} %copy-done.2, s32[2048]{0:T(1024)S(1)} %bitcast.313, f32[2048,9]{1,0:T(8,128)S(1)} %copy.233), kind=kCustom, calls=%fused_computation.4.clone.clone.1 | custom fusion | flops 18432 | bytes 229376 | tf_op jit(solution)/shard_map/while/body/eval_jaxpr/scatter-add | solution.py:197
  484.1 7.0 gather_fusion
  496.2 4.7 fusion.184
  508.8 6.0 fusion.186
  514.8 9.6 fusion.187
  529.5 7.6 fusion.188
  538.6 12.2 %scatter_fusion = f32[9,4096]{0,1:T(8,128)S(1)} fusion(f32[9,4096]{0,1:T(8,128)S(1)} %copy-done.2, s32[2048]{0:T(1024)S(1)} %bitcast.313, f32[2048,9]{1,0:T(8,128)S(1)} %copy.233), kind=kCustom, calls=%fused_computation.4.clone.clone.1 | custom fusion | flops 18432 | bytes 229376 | tf_op jit(solution)/shard_map/while/body/eval_jaxpr/scatter-add | solution.py:197
  552.9 7.0 gather_fusion
  565.0 4.7 fusion.184
  577.6 6.0 fusion.186
  583.6 9.6 fusion.187
  598.2 7.6 fusion.188
  607.4 12.2 %scatter_fusion = f32[9,4096]{0,1:T(8,128)S(1)} fusion(f32[9,4096]{0,1:T(8,128)S(1)} %copy-done.2, s32[2048]{0:T(1024)S(1)} %bitcast.313, f32[2048,9]{1,0:T(8,128)S(1)} %copy.233), kind=kCustom, calls=%fused_computation.4.clone.clone.1 | custom fusion | flops 18432 | bytes 229376 | tf_op jit(solution)/shard_map/while/body/eval_jaxpr/scatter-add | solution.py:197
  621.7 7.0 gather_fusion
  633.7 4.7 fusion.184
  646.4 6.0 fusion.186
  652.4 9.6 fusion.187
  667.0 7.6 fusion.188
  676.2 12.2 %scatter_fusion = f32[9,4096]{0,1:T(8,128)S(1)} fusion(f32[9,4096]{0,1:T(8,128)S(1)} %copy-done.2, s32[2048]{0:T(1024)S(1)} %bitcast.313, f32[2048,9]{1,0:T(8,128)S(1)} %copy.233), kind=kCustom, calls=%fused_computation.4.clone.clone.1 | custom fusion | flops 18432 | bytes 229376 | tf_op jit(solution)/shard_map/while/body/eval_jaxpr/scatter-add | solution.py:197
  690.5 7.0 gather_fusion
  702.6 4.7 fusion.184
  715.2 6.0 fusion.186
  721.2 9.6 fusion.187
  735.8 7.6 fusion.188
  745.0 12.2 %scatter_fusion = f32[9,4096]{0,1:T(8,128)S(1)} fusion(f32[9,4096]{0,1:T(8,128)S(1)} %copy-done.2, s32[2048]{0:T(1024)S(1)} %bitcast.313, f32[2048,9]{1,0:T(8,128)S(1)} %copy.233), kind=kCustom, calls=%fused_computation.4.clone.clone.1 | custom fusion | flops 18432 | bytes 229376 | tf_op jit(solution)/shard_map/while/body/eval_jaxpr/scatter-add | solution.py:197
  759.3 7.0 gather_fusion
  771.3 4.7 fusion.184
  784.0 6.0 fusion.186
  790.0 9.6 fusion.187
  804.6 7.6 fusion.188
  813.8 12.2 %scatter_fusion = f32[9,4096]{0,1:T(8,128)S(1)} fusion(f32[9,4096]{0,1:T(8,128)S(1)} %copy-done.2, s32[2048]{0:T(1024)S(1)} %bitcast.313, f32[2048,9]{1,0:T(8,128)S(1)} %copy.233), kind=kCustom, calls=%fused_computation.4.clone.clone.1 | custom fusion | flops 18432 | bytes 229376 | tf_op jit(solution)/shard_map/while/body/eval_jaxpr/scatter-add | solution.py:197
  828.1 7.0 gather_fusion
  840.1 4.7 fusion.184
  852.8 6.0 fusion.186
  858.8 9.6 fusion.187
  873.4 7.6 fusion.188
  882.6 12.2 %scatter_fusion = f32[9,4096]{0,1:T(8,128)S(1)} fusion(f32[9,4096]{0,1:T(8,128)S(1)} %copy-done.2, s32[2048]{0:T(1024)S(1)} %bitcast.313, f32[2048,9]{1,0:T(8,128)S(1)} %copy.233), kind=kCustom, calls=%fused_computation.4.clone.clone.1 | custom fusion | flops 18432 | bytes 229376 | tf_op jit(solution)/shard_map/while/body/eval_jaxpr/scatter-add | solution.py:197
  911.3 3.8 broadcast_multiply_fusion.10
  917.0 3.4 fusion.80
  922.7 4.2 all-to-all-start.1
  927.0 15.2 %all-to-all-done.1 = f32[59,8,512]{2,0,1:T(8,128)S(1)} async-done(((f32[59,8,512]{2,0,1:T(8,128)}), f32[59,8,512]{2,0,1:T(8,128)S(1)}, u32[]{:S(2)}, u32[]{:S(2)}) %all-to-all-start.1) | async-done | bytes 966688 | tf_op jit(solution)/shard_map/all_to_all | solution.py:230
  945.4 15.5 %scatter_fusion.1 = f32[256,59,32]{1,2,0:T(8,128)} fusion(f32[256,59,32]{1,2,0:T(8,128)} %broadcast_in_dim.76, s32[128]{0:T(128)S(1)} %reshape.6860, f32[128,59,32]{1,2,0:T(8,128)S(1)} %bitcast.272), kind=kCustom, calls=%fused_computation.5 | custom fusion | flops 241664 | bytes 2900480 | tf_op jit(solution)/shard_map/scatter-add | solution.py:236
  961.0 3.8 copy.154
  966.4 147.6 %all-gather.2.cloned.1.call-done = f32[4,59,8192]{2,1,0:T(8,128)} async-done(((f32[1,59,8192]{2,1,0:T(8,128)}), f32[4,59,8192]{2,1,0:T(8,128)}) %all-gather.2.cloned.1.call-update) | async-done | bytes 7733264 | tf_op jit(solution)/shard_map/all_gather | solution.py:238
  1114.0 5.5 reduce_sum.117
  (961 shorter events, 213.5 us)
Async XLA Ops:
  17.3 8.4 copy-start.119
  17.3 8.5 copy-start.120
  17.3 9.8 copy-start.52
  20.5 289.6 %all-to-all-start = ((f32[59,8,512]{2,0,1:T(8,128)}), f32[59,8,512]{2,0,1:T(8,128)S(1)}, u32[]{:S(2)}, u32[]{:S(2)}) async-start(f32[59,8,512]{2,0,1:T(8,128)} %copy.136), calls=%async_computation | async-start | bytes 2097152 | tf_op jit(solution)/shard_map/all_to_all | solution.py:224
  177.9 129.5 %copy-start.117 = (f32[1,32,3,256]{3,1,2,0:T(8,128)S(1)}, f32[1,32,3,256]{3,1,2,0:T(8,128)}, u32[]{:S(2)}) copy-start(f32[1,32,3,256]{3,1,2,0:T(8,128)} %param.10) | copy-start | bytes 294916
  311.0 9.6 copy-start.53
  311.0 9.6 copy-start.55
  311.0 9.6 copy-start.57
  311.0 9.6 copy-start.59
  311.0 15.2 %copy-start.28 = (f32[1,8,512]{2,0,1:T(1,128)}, f32[1,8,512]{2,0,1:T(1,128)S(1)}, u32[]{:S(2)}) copy-start(f32[1,8,512]{2,0,1:T(1,128)S(1)} %get-tuple-element.421) | copy-start | bytes 49156
  312.5 10.4 copy-start.14
  313.8 8.9 copy-start.12
  313.8 12.4 %copy-start.50 = (f32[1,8,512]{2,0,1:T(1,128)}, f32[1,8,512]{2,0,1:T(1,128)S(1)}, u32[]{:S(2)}) copy-start(f32[1,8,512]{2,0,1:T(1,128)S(1)} %get-tuple-element.422) | copy-start | bytes 49156
  320.4 5.9 copy-start.77
  320.4 5.9 copy-start.79
  320.4 5.9 copy-start.81
  320.5 5.9 copy-start.83
  320.5 5.9 copy-start.85
  320.5 5.9 copy-start.87
  320.5 5.9 copy-start.89
  320.5 5.9 copy-start.91
  320.5 5.9 copy-start.93
  391.9 7.7 copy-start.31
  460.7 7.7 copy-start.31
  529.5 7.7 copy-start.31
  598.2 7.7 copy-start.31
  667.0 7.7 copy-start.31
  735.8 7.7 copy-start.31
  804.6 7.7 copy-start.31
  873.4 7.7 copy-start.31
  896.3 12.2 %copy-start.40 = (f32[1,4096]{1,0:T(1,128)S(1)}, f32[1,4096]{1,0:T(1,128)}, u32[]{:S(2)}) copy-start(f32[1,4096]{1,0:T(1,128)} %get-tuple-element.308) | copy-start | bytes 49156
  896.3 13.0 %copy-start.33 = (f32[1,4096]{1,0:T(1,128)S(1)}, f32[1,4096]{1,0:T(1,128)}, u32[]{:S(2)}) copy-start(f32[1,4096]{1,0:T(1,128)} %copy-done.32) | copy-start | bytes 49156
  896.3 13.0 %copy-start.35 = (f32[1,4096]{1,0:T(1,128)S(1)}, f32[1,4096]{1,0:T(1,128)}, u32[]{:S(2)}) copy-start(f32[1,4096]{1,0:T(1,128)} %copy-done.34) | copy-start | bytes 49156
  896.3 13.0 %copy-start.37 = (f32[1,4096]{1,0:T(1,128)S(1)}, f32[1,4096]{1,0:T(1,128)}, u32[]{:S(2)}) copy-start(f32[1,4096]{1,0:T(1,128)} %copy-done.36) | copy-start | bytes 49156
  896.3 13.0 %copy-start.39 = (f32[1,4096]{1,0:T(1,128)S(1)}, f32[1,4096]{1,0:T(1,128)}, u32[]{:S(2)}) copy-start(f32[1,4096]{1,0:T(1,128)} %copy-done.38) | copy-start | bytes 49156
  896.3 13.0 %copy-start.45 = (f32[1,4096]{1,0:T(1,128)S(1)}, f32[1,4096]{1,0:T(1,128)}, u32[]{:S(2)}) copy-start(f32[1,4096]{1,0:T(1,128)} %copy-done.44) | copy-start | bytes 49156
  896.3 13.0 %copy-start.47 = (f32[1,4096]{1,0:T(1,128)S(1)}, f32[1,4096]{1,0:T(1,128)}, u32[]{:S(2)}) copy-start(f32[1,4096]{1,0:T(1,128)} %copy-done.46) | copy-start | bytes 49156
  896.4 13.0 %copy-start.49 = (f32[1,4096]{1,0:T(1,128)S(1)}, f32[1,4096]{1,0:T(1,128)}, u32[]{:S(2)}) copy-start(f32[1,4096]{1,0:T(1,128)} %copy-done.48) | copy-start | bytes 49156
  898.6 12.4 %copy-start.41 = (f32[1,4096]{1,0:T(1,128)S(1)}, f32[1,4096]{1,0:T(1,128)}, u32[]{:S(2)}) copy-start(f32[1,4096]{1,0:T(1,128)} %get-tuple-element.327) | copy-start | bytes 49156
  898.6 12.4 %copy-start.42 = (f32[1,4096]{1,0:T(1,128)S(1)}, f32[1,4096]{1,0:T(1,128)}, u32[]{:S(2)}) copy-start(f32[1,4096]{1,0:T(1,128)} %get-tuple-element.333) | copy-start | bytes 49156
  898.6 12.4 %copy-start.43 = (f32[1,4096]{1,0:T(1,128)S(1)}, f32[1,4096]{1,0:T(1,128)}, u32[]{:S(2)}) copy-start(f32[1,4096]{1,0:T(1,128)} %get-tuple-element.339) | copy-start | bytes 49156
  898.7 12.4 %copy-start.51 = (f32[1,8,512]{2,0,1:T(1,128)S(1)}, f32[1,8,512]{2,0,1:T(1,128)}, u32[]{:S(2)}) copy-start(f32[1,8,512]{2,0,1:T(1,128)} %copy-done.50) | copy-start | bytes 49156
  898.7 12.4 %copy-start.70 = (f32[1,8,512]{2,0,1:T(1,128)S(1)}, f32[1,8,512]{2,0,1:T(1,128)}, u32[]{:S(2)}) copy-start(f32[1,8,512]{2,0,1:T(1,128)} %copy-done.69) | copy-start | bytes 49156
  898.7 12.4 %copy-start.72 = (f32[1,8,512]{2,0,1:T(1,128)S(1)}, f32[1,8,512]{2,0,1:T(1,128)}, u32[]{:S(2)}) copy-start(f32[1,8,512]{2,0,1:T(1,128)} %copy-done.71) | copy-start | bytes 49156
  898.7 12.4 %copy-start.74 = (f32[1,8,512]{2,0,1:T(1,128)S(1)}, f32[1,8,512]{2,0,1:T(1,128)}, u32[]{:S(2)}) copy-start(f32[1,8,512]{2,0,1:T(1,128)} %copy-done.73) | copy-start | bytes 49156
  898.7 12.4 %copy-start.76 = (f32[1,8,512]{2,0,1:T(1,128)S(1)}, f32[1,8,512]{2,0,1:T(1,128)}, u32[]{:S(2)}) copy-start(f32[1,8,512]{2,0,1:T(1,128)} %copy-done.75) | copy-start | bytes 49156
  898.7 12.4 %copy-start.78 = (f32[1,8,512]{2,0,1:T(1,128)S(1)}, f32[1,8,512]{2,0,1:T(1,128)}, u32[]{:S(2)}) copy-start(f32[1,8,512]{2,0,1:T(1,128)} %copy-done.77) | copy-start | bytes 49156
  898.7 12.4 %copy-start.80 = (f32[1,8,512]{2,0,1:T(1,128)S(1)}, f32[1,8,512]{2,0,1:T(1,128)}, u32[]{:S(2)}) copy-start(f32[1,8,512]{2,0,1:T(1,128)} %copy-done.79) | copy-start | bytes 49156
  898.7 12.4 %copy-start.82 = (f32[1,8,512]{2,0,1:T(1,128)S(1)}, f32[1,8,512]{2,0,1:T(1,128)}, u32[]{:S(2)}) copy-start(f32[1,8,512]{2,0,1:T(1,128)} %copy-done.81) | copy-start | bytes 49156
  898.7 12.4 %copy-start.84 = (f32[1,8,512]{2,0,1:T(1,128)S(1)}, f32[1,8,512]{2,0,1:T(1,128)}, u32[]{:S(2)}) copy-start(f32[1,8,512]{2,0,1:T(1,128)} %copy-done.83) | copy-start | bytes 49156
  898.7 12.4 %copy-start.86 = (f32[1,8,512]{2,0,1:T(1,128)S(1)}, f32[1,8,512]{2,0,1:T(1,128)}, u32[]{:S(2)}) copy-start(f32[1,8,512]{2,0,1:T(1,128)} %copy-done.85) | copy-start | bytes 49156
  898.8 12.4 %copy-start.88 = (f32[1,8,512]{2,0,1:T(1,128)S(1)}, f32[1,8,512]{2,0,1:T(1,128)}, u32[]{:S(2)}) copy-start(f32[1,8,512]{2,0,1:T(1,128)} %copy-done.87) | copy-start | bytes 49156
  898.8 12.4 %copy-start.90 = (f32[1,8,512]{2,0,1:T(1,128)S(1)}, f32[1,8,512]{2,0,1:T(1,128)}, u32[]{:S(2)}) copy-start(f32[1,8,512]{2,0,1:T(1,128)} %copy-done.89) | copy-start | bytes 49156
  898.8 12.4 %copy-start.92 = (f32[1,8,512]{2,0,1:T(1,128)S(1)}, f32[1,8,512]{2,0,1:T(1,128)}, u32[]{:S(2)}) copy-start(f32[1,8,512]{2,0,1:T(1,128)} %copy-done.91) | copy-start | bytes 49156
  898.8 12.4 %copy-start.94 = (f32[1,8,512]{2,0,1:T(1,128)S(1)}, f32[1,8,512]{2,0,1:T(1,128)}, u32[]{:S(2)}) copy-start(f32[1,8,512]{2,0,1:T(1,128)} %copy-done.93) | copy-start | bytes 49156
  899.9 9.5 copy-start.100
  899.9 11.4 %copy-start.96 = (f32[1,8,512]{2,0,1:T(1,128)S(1)}, f32[1,8,512]{2,0,1:T(1,128)}, u32[]{:S(2)}) copy-start(f32[1,8,512]{2,0,1:T(1,128)} %copy-done.95) | copy-start | bytes 49156
  899.9 11.4 %copy-start.98 = (f32[1,8,512]{2,0,1:T(1,128)S(1)}, f32[1,8,512]{2,0,1:T(1,128)}, u32[]{:S(2)}) copy-start(f32[1,8,512]{2,0,1:T(1,128)} %copy-done.97) | copy-start | bytes 49156
  899.9 11.4 %copy-start.101 = (f32[1,4096]{1,0:T(1,128)S(1)}, f32[1,4096]{1,0:T(1,128)}, u32[]{:S(2)}) copy-start(f32[1,4096]{1,0:T(1,128)} %get-tuple-element.303) | copy-start | bytes 49156
  900.9 10.4 copy-start.102
  901.9 9.4 copy-start.103
  901.9 9.4 copy-start.105
  922.7 19.6 %all-to-all-start.1 = ((f32[59,8,512]{2,0,1:T(8,128)}), f32[59,8,512]{2,0,1:T(8,128)S(1)}, u32[]{:S(2)}, u32[]{:S(2)}) async-start(f32[59,8,512]{2,0,1:T(8,128)} %copy.152), calls=%async_computation.1 | async-start | bytes 2097152 | tf_op jit(solution)/shard_map/all_to_all | solution.py:230
  926.9 187.1 %all-gather.2.cloned.1.call-start = ((), (), s32[]{:S(2)}) async-start(), calls=%async_computation.2 | async-start | bytes 10485760 | tf_op jit(solution)/shard_map/all_gather | solution.py:238
  (186 other events, 451.2 us)
Sparse Core Ops, SparseCore 0:
  964.9 148.9 all-gather.1
